TPU v7x, 512 devices: a whole 4x8x8 slice. The times are simulated.
512 devices in a mesh: dp: 16 (over z, core), tp: 32 (over y, x).
Axes of the slice: x: 4, y: 8, z: 8, core: 2. Of those that a mesh axis runs over, the one named last changes fastest.
Arguments:
- q_new: bfloat16 [512, 1536], P(('dp', 'tp'))
- new_key_value: bfloat16 [512, 512], P(('dp', 'tp')), may hold values from -6 to 6
- resid_dec: bfloat16 [512, 1536], P(('dp', 'tp')), may hold values from -6 to 6
- placing: int32 [512], replicated, may hold values from 0 to 511, as said below
- lengths: int32 [512], P('dp'), may hold values from 5 to 2048, as said below
- write_pos: int32 [512], P('dp'), may hold values from 4 to 2047, as said below
- k_cache: bfloat16 [512, 2, 2048, 128], P('dp', None, 'tp')
- value_cache: bfloat16 [512, 2, 2048, 128], P('dp', None, 'tp'), may hold values from -6 to 6
- w_out: bfloat16 [1536, 1536], P(None, 'tp'), may hold values from -0.15625 to 0.15625
- x_pre: bfloat16 [32256, 1536], P(('dp', 'tp')), may hold values from -6 to 6
- routes: int32 [32768, 4], P(('dp', 'tp')), may hold values from 0 to 31, all different within a row; in each aligned block of 64 rows (0 to 63, 64 to 127, ...) at most 16 rows name the same one
- route_scale: float32 [32768, 4], P(('dp', 'tp')), may hold values from 0.2 to 2
- moe_gain: float32 [1536], replicated, may hold values from 0.5 to 1.5
- w_gate: bfloat16 [32, 768, 1536], P('tp', 'dp'), may hold values from -0.15625 to 0.15625
- w_up: bfloat16 [32, 768, 1536], P('tp', 'dp'), may hold values from -0.15625 to 0.15625
- w_down: bfloat16 [32, 768, 1536], P('tp', 'dp'), may hold values from -0.21875 to 0.21875
Outputs:
- out_pre: bfloat16 [32256, 1536], P(('dp', 'tp'))
- out_dec: bfloat16 [512, 1536], P(('dp', 'tp'))
Inputs may be any that keep to these rules, and one draw needn't show every extreme that they name: Each of 0 to 511 appears once; cache row j belongs to request placing[j]. `lengths`: a cache row is either full (2048 live slots) or filled from slot 0 up; some row is full. `write_pos`: below the row's length; a row that is not full writes at its length - 1, a full row anywhere past the sink slots. `routes`: the 64 rows of one device name any one expert at most 16 times.
All inputs are finite; a program needn't handle non-finite values.
Results may differ from a plain program's by a relative error of at most 0.007.
Values may be sent and summed in bfloat16 or wider, within the bound.
No kernel may reach another device: no remote copies, remote signals or barrier semaphores. Data moves between devices by JAX's collectives and lax.ppermute only.
A program may use at most 64 MiB of HBM per device.

v0:
```python
import jax
import jax.numpy as jnp
from jax import lax
from jax.sharding import Mesh
from jax.sharding import PartitionSpec as P

TP = ("y", "x")
F32 = jnp.float32
BF16 = jnp.bfloat16


def contract_rows(left_rows, unit_rows):
    return lax.dot_general(
        left_rows, unit_rows, (((1,), (1,)), ((), ())), preferred_element_type=F32
    )


def swap(blocks, axis_name):
    return lax.all_to_all(blocks, axis_name, split_axis=0, concat_axis=0, tiled=True)


def choose_rows(table, rows):
    return jnp.dot(table.astype(BF16), rows, preferred_element_type=F32).astype(BF16)


def pieces_of(x):
    high = lax.reduce_precision(x, 8, 7)
    middle = lax.reduce_precision(x - high, 8, 7)
    low = lax.reduce_precision(x - high - middle, 8, 7)
    return (high.astype(BF16), middle.astype(BF16), low.astype(BF16))


def rms(rows_f32, gain):
    mean_square = jnp.mean(rows_f32 * rows_f32, axis=-1, keepdims=True)
    return (rows_f32 * lax.rsqrt(mean_square + 1e-06) * gain).astype(BF16)


def sum_and_copy(parts, copies):
    count, rows, columns = parts.shape
    same = jnp.arange(copies * rows, dtype=jnp.int32)[:, None] % rows
    same = same == jnp.arange(count * rows, dtype=jnp.int32)[None, :] % rows
    return choose_rows(same, parts.reshape(count * rows, columns)).reshape(copies, rows, columns)


def expert_units(rows, units, gate):
    upper = contract_rows(rows, units[1])
    active = (jnp.maximum(gate, 0.0) * upper).astype(BF16)
    return jnp.dot(active, units[2], preferred_element_type=F32).astype(BF16)


def on_device(
    q_new,
    new_key_value,
    resid_dec,
    placing,
    lengths,
    write_pos,
    k_cache,
    value_cache,
    w_out,
    x_pre,
    routes,
    route_scale,
    moe_gain,
    w_gate,
    w_up,
    w_down,
):
    dp_size = lax.axis_size("dp")
    lines, posts = (lax.axis_size("y"), lax.axis_size("x"))
    tp_size = lines * posts
    dp_group = lax.axis_index("dp")
    line = lax.axis_index("y")
    tp_lane = line * posts + lax.axis_index("x")
    group_reqs, kv_heads, slot_dev, head_size = k_cache.shape
    width = q_new.shape[1]
    heads = width // head_size
    per_group = heads // kv_heads
    total_reqs = placing.shape[0]
    experts = tp_size * w_gate.shape[0]
    assert group_reqs == tp_size and experts == tp_size
    no_value = jnp.zeros((), BF16)
    rows_dev, top_count = routes.shape
    pre_rows = rows_dev - 1
    capacity = min(2 * rows_dev * top_count // experts, rows_dev)
    route_weight = route_scale / jnp.sum(route_scale, axis=-1, keepdims=True)
    expert_ids = jnp.arange(experts, dtype=jnp.int32)
    hits = routes[:, :, None] == expert_ids[None, None, :]
    weight_of = jnp.sum(jnp.where(hits, route_weight[:, :, None], 0.0), axis=1)
    routed = jnp.any(hits[:pre_rows], axis=1)
    row_ids = jnp.arange(pre_rows, dtype=jnp.int32)
    before = (row_ids[None, :] < row_ids[:, None]).astype(BF16)
    position = jnp.dot(before, routed.astype(BF16), preferred_element_type=F32).astype(jnp.int32)
    slots = jnp.arange(capacity, dtype=jnp.int32)
    pick = routed[:, :, None] & (position[:, :, None] == slots[None, None, :])
    pick_table = pick.reshape(pre_rows, experts * capacity)
    x_f32 = x_pre.astype(F32)
    outgoing = lax.dot_general(
        pick_table.astype(BF16),
        lax.optimization_barrier(rms(x_f32, moe_gain)),
        (((0,), (0,)), ((), ())),
        preferred_element_type=F32,
    ).astype(BF16)
    stored, outgoing = lax.optimization_barrier(((w_gate, w_up, w_down), outgoing))
    units = lax.all_gather(jnp.concatenate(stored, axis=0), "dp", axis=1, tiled=True)
    columns = heads + 2 * kv_heads
    share = columns * head_size // posts
    post = lax.axis_index("x")
    fresh = jnp.concatenate([q_new, new_key_value], axis=1)
    fresh, outgoing = lax.optimization_barrier((fresh, outgoing))
    received = swap(outgoing.reshape(experts, capacity, width), TP)
    line_fresh = lax.all_gather(fresh, "x", axis=0, tiled=True)
    line_share = lax.dynamic_slice_in_dim(line_fresh, post * share, share, axis=1)
    all_rows = lax.all_gather(line_share, "dp", axis=0, tiled=True)
    wanted = lax.dynamic_slice_in_dim(placing, dp_group * group_reqs, group_reqs)
    held = jnp.arange(dp_size, dtype=jnp.int32)[:, None] * tp_size + line * posts
    held = (held + jnp.arange(posts, dtype=jnp.int32)[None, :]).reshape(1, dp_size * posts)
    mine = choose_rows(jnp.tile(wanted, lines)[:, None] == held, all_rows)
    mine, received = lax.optimization_barrier((mine, received))
    chosen = swap(mine.reshape(lines, group_reqs, share), "y")
    cached = swap(sum_and_copy(chosen, posts), "x").reshape(
        posts, group_reqs, columns // posts, head_size
    )
    cached = jnp.transpose(cached, (1, 0, 2, 3)).reshape(group_reqs, columns, head_size)
    query_head_list = cached[:, :heads].reshape(group_reqs, kv_heads, per_group, head_size)
    incoming_key = cached[:, heads : heads + kv_heads][:, :, None, :]
    incoming_value = cached[:, heads + kv_heads :][:, :, None, :]
    slot_ids = tp_lane * slot_dev + jnp.arange(slot_dev, dtype=jnp.int32)
    written = (slot_ids[None, :] == write_pos[:, None])[:, None, :, None]
    key_rows = jnp.where(written, incoming_key, k_cache)
    value_rows = jnp.where(written, incoming_value, value_cache)
    scores = jnp.einsum(
        "rgqd,rgsd->rgqs", query_head_list, key_rows, preferred_element_type=F32
    ) * head_size ** (-0.5)
    is_valid = (slot_ids[None, :] < lengths[:, None])[:, None, None, :]
    masked = jnp.where(is_valid, scores, -1e30)
    local_peak = jnp.max(masked, axis=-1)
    weights = jnp.where(is_valid, jnp.exp(masked - local_peak[..., None]), 0.0)
    local_total = jnp.sum(weights, axis=-1)
    high = lax.reduce_precision(weights, 8, 7)
    halves = jnp.concatenate([high, weights - high], axis=2).astype(BF16)
    local_mixed = jnp.einsum("rgqs,rgsd->rgqd", halves, value_rows, preferred_element_type=F32)
    local_mixed = local_mixed[:, :, :per_group] + local_mixed[:, :, per_group:]

    def lane_row(values):
        row = jnp.concatenate(pieces_of(values.reshape(group_reqs, heads)), axis=1)
        return jnp.pad(row, ((0, 0), (0, head_size - row.shape[1])))[:, None, :]

    parts = jnp.concatenate(
        [
            local_mixed.reshape(group_reqs, heads, head_size).astype(BF16),
            lane_row(local_peak),
            lane_row(local_total),
            jnp.zeros((group_reqs, 2, head_size), BF16),
        ],
        axis=1,
    )
    gathered = swap(parts, TP)
    arrived = received.reshape(experts * capacity, width)
    gathered, gate = lax.optimization_barrier((gathered, contract_rows(arrived, units[0])))
    tail = gathered[:, heads : heads + 2, : 3 * heads].astype(F32)
    tail = tail[..., :heads] + tail[..., heads : 2 * heads] + tail[..., 2 * heads :]
    peaks, totals = (tail[:, 0], tail[:, 1])
    scale = jnp.exp(peaks - jnp.max(peaks, axis=0, keepdims=True))
    total = jnp.sum(scale * totals, axis=0)
    mixed = jnp.sum(scale[:, :, None] * gathered[:, :heads].astype(F32), axis=0)
    attention_row = (mixed / total[:, None]).astype(BF16)
    rows = jnp.concatenate([attention_row, resid_dec.reshape(heads, head_size)], axis=0)
    group_rows = swap(jnp.broadcast_to(rows[None], (tp_size,) + rows.shape), TP)
    pre_out = expert_units(arrived, units, gate)
    group_rows, pre_out = lax.optimization_barrier((group_rows, pre_out))
    returned = swap(pre_out.reshape(experts, capacity, width), TP)
    attention = group_rows[:, :heads].reshape(group_reqs, width)
    resid_rows = group_rows[:, heads:].reshape(group_reqs, width)
    projected = jnp.dot(attention, w_out, preferred_element_type=F32).astype(BF16)
    all_projected = lax.all_gather(projected, "dp", axis=0, tiled=True)
    home_ids = dp_group * group_reqs + jnp.arange(group_reqs, dtype=jnp.int32)
    at_home = choose_rows(home_ids[:, None] == placing[None, :], all_projected)
    at_home, returned = lax.optimization_barrier((at_home, returned))
    packed = at_home.reshape(heads, head_size)
    packed = swap(jnp.broadcast_to(packed[None], (tp_size,) + packed.shape), TP)
    proj_home = packed.reshape(tp_size, group_reqs, width // tp_size)
    proj_home = jnp.transpose(proj_home, (1, 0, 2)).reshape(group_reqs, width)
    proj_home = lax.optimization_barrier(proj_home)
    hidden_all = (resid_rows.astype(F32) + proj_home.astype(F32)).astype(BF16)
    own_row = lax.dynamic_slice_in_dim(hidden_all, tp_lane, 1)
    normed_dec = rms(hidden_all.astype(F32), moe_gain)
    dec_out = expert_units(normed_dec, units, contract_rows(normed_dec, units[0]))
    own_row, dec_out = lax.optimization_barrier((own_row, dec_out))
    dec_back = swap(dec_out.reshape(group_reqs, heads, head_size), TP).astype(F32)
    dec_weight = weight_of[pre_rows:].reshape(experts, 1, 1)
    dec_mixture = jnp.sum(dec_weight * dec_back, axis=0).reshape(1, width)
    out_dec = (own_row.astype(F32) + dec_mixture).astype(BF16)
    flat_back = returned.reshape(experts * capacity, width)
    high, middle, low = pieces_of(weight_of[:pre_rows])

    def mix(piece):
        table = jnp.where(pick, piece[:, :, None], no_value)
        return jnp.dot(
            table.reshape(pre_rows, experts * capacity), flat_back, preferred_element_type=F32
        )

    out_pre = (x_f32 + (mix(high) + mix(middle) + mix(low))).astype(BF16)
    return (out_pre, out_dec)


def solution(mesh):
    groups, lanes = mesh.devices.shape
    lines = min(8, groups)
    fine = Mesh(mesh.devices.reshape(groups, lines, lanes // lines), ("dp", "y", "x"))
    rows = P(("dp", "y", "x"), None)
    units = P(TP, "dp", None)
    cache = P("dp", None, TP, None)
    placed = (rows, rows, rows, P(), P("dp"), P("dp"), cache, cache, P(None, TP))
    placed = placed + (rows, rows, rows, P(), units, units, units)
    return jax.shard_map(
        on_device, mesh=fine, in_specs=placed, out_specs=(rows, rows), check_vma=False
    )
```

profile of v0, /device:TPU:8, one launch (start us, length us, event | category | flops | bytes accessed | tf_op | source)
XLA Modules:
  0.0 216.4 jit_solution(434798193457296705)
XLA Ops:
  7.3 0.8 iota_compare_fusion.1
  8.3 1.1 fusion.20
  9.4 1.1 fusion.22
  10.5 0.1 fusion.32
  10.6 1.8 convolution_convert_fusion.1
  12.4 0.8 pad_maximum_fusion
  13.3 10.2 %all-to-all-start = ((bf16[32,16,1536]{2,1,0:T(8,128)(2,1)}), bf16[32,16,1536]{2,1,0:T(8,128)(2,1)S(1)}, u32[]{:S(2)}, u32[]{:S(2)}) async-start(bf16[32,16,1536]{2,1,0:T(8,128)(2,1)} %bitcast.3), calls=%async_computation | async-start | bytes 3145728 | tf_op jit(solution)/shard_map/all_to_all | solution.py:19
  23.6 12.4 %all-gather = bf16[4,1,2048]{2,1,0:T(2,128)(2,1)S(1)} all-gather(bf16[1,1,2048]{2,1,0:T(2,128)(2,1)S(1)} %bitcast.119), channel_id=1, replica_groups=mesh['dp'=16,'y'=8,'x'=4] {'x'}, dimensions={0}, use_global_device_ids=true | all-gather | bytes 20480 | tf_op jit(solution)/shard_map/all_gather | solution.py:112
  36.0 23.4 %all-gather.1 = bf16[16,4,512]{2,1,0:T(4,128)(2,1)S(1)} all-gather(bf16[1,4,512]{2,1,0:T(4,128)(2,1)S(1)} %bitcast.121), channel_id=1, replica_groups=mesh['dp'=16,'y'=8,'x'=4] {'dp'}, dimensions={0}, use_global_device_ids=true | all-gather | bytes 69632 | tf_op jit(solution)/shard_map/all_gather | solution.py:114
  59.8 1.0 convolution_convert_fusion.3
  60.8 1.1 all-to-all-done
  61.9 8.0 %all-to-all-start.1 = ((bf16[8,32,512]{2,1,0:T(8,128)(2,1)}), bf16[8,32,512]{2,1,0:T(8,128)(2,1)S(1)}, u32[]{:S(2)}, u32[]{:S(2)}) async-start(bf16[8,32,512]{2,1,0:T(8,128)(2,1)} %bitcast.4), calls=%async_computation.1 | async-start | bytes 524288 | tf_op jit(solution)/shard_map/all_to_all | solution.py:19
  69.9 10.9 %all-to-all-done.1 = bf16[8,32,512]{2,1,0:T(8,128)(2,1)S(1)} async-done(((bf16[8,32,512]{2,1,0:T(8,128)(2,1)}), bf16[8,32,512]{2,1,0:T(8,128)(2,1)S(1)}, u32[]{:S(2)}, u32[]{:S(2)}) %all-to-all-start.1) | async-done | bytes 262176 | tf_op jit(solution)/shard_map/all_to_all | solution.py:19
  80.8 0.9 convolution_convert_fusion.4
  81.7 3.3 %all-to-all-start.2 = ((bf16[4,32,512]{2,1,0:T(8,128)(2,1)}), bf16[4,32,512]{2,1,0:T(8,128)(2,1)S(1)}, u32[]{:S(2)}, u32[]{:S(2)}) async-start(bf16[4,32,512]{2,1,0:T(8,128)(2,1)} %bitcast.6), calls=%async_computation.2 | async-start | bytes 262144 | tf_op jit(solution)/shard_map/all_to_all | solution.py:19
  85.3 5.7 %all-to-all-done.2 = bf16[4,32,512]{2,1,0:T(8,128)(2,1)S(1)} async-done(((bf16[4,32,512]{2,1,0:T(8,128)(2,1)}), bf16[4,32,512]{2,1,0:T(8,128)(2,1)S(1)}, u32[]{:S(2)}, u32[]{:S(2)}) %all-to-all-start.2) | async-done | bytes 131104 | tf_op jit(solution)/shard_map/all_to_all | solution.py:19
  91.1 1.1 fusion.83
  92.3 0.3 reduce-precision_convert_fusion
  92.6 1.7 fusion.12
  94.9 0.7 copy.83
  95.6 5.0 %all-to-all-start.3 = ((bf16[32,16,128]{2,1,0:T(8,128)(2,1)}), bf16[32,16,128]{2,1,0:T(8,128)(2,1)S(1)}, u32[]{:S(2)}, u32[]{:S(2)}) async-start(bf16[32,16,128]{2,1,0:T(8,128)(2,1)} %copy.83), calls=%async_computation.3 | async-start | bytes 262144 | tf_op jit(solution)/shard_map/all_to_all | solution.py:19
  100.6 4.3 %fusion.5 = f32[512,768]{1,0:T(8,128)} fusion(bf16[512,1536]{1,0:T(8,128)(2,1)S(1)} %bitcast.106, bf16[3,768,1536]{2,1,0:T(8,128)(2,1)} %all-gather.4.cloned.1.call-done), kind=kOutput, calls=%fused_computation.14 | convolution fusion | flops 1207959552 | bytes 5505024 | tf_op jit(solution)/shard_map/dot_general | solution.py:13
  104.9 5.3 %all-to-all-done.3 = bf16[32,16,128]{2,1,0:T(8,128)(2,1)S(1)} async-done(((bf16[32,16,128]{2,1,0:T(8,128)(2,1)}), bf16[32,16,128]{2,1,0:T(8,128)(2,1)S(1)}, u32[]{:S(2)}, u32[]{:S(2)}) %all-to-all-start.3) | async-done | bytes 131104 | tf_op jit(solution)/shard_map/all_to_all | solution.py:19
  110.7 0.7 broadcast_in_dim.147
  111.4 4.7 %all-to-all-start.4 = ((bf16[32,24,128]{2,1,0:T(8,128)(2,1)}), bf16[32,24,128]{2,1,0:T(8,128)(2,1)S(1)}, u32[]{:S(2)}, u32[]{:S(2)}) async-start(bf16[32,24,128]{2,1,0:T(8,128)(2,1)} %broadcast_in_dim.147), calls=%async_computation.4 | async-start | bytes 393216 | tf_op jit(solution)/shard_map/all_to_all | solution.py:19
  116.1 7.2 %convolution_convert_fusion = bf16[512,1536]{1,0:T(8,128)(2,1)} fusion(bf16[3,768,1536]{2,1,0:T(8,128)(2,1)} %all-gather.4.cloned.1.call-done, f32[512,768]{1,0:T(8,128)} %fusion.5, bf16[512,1536]{1,0:T(8,128)(2,1)S(1)} %bitcast.107), kind=kOutput, calls=%fused_computation | convolution fusion | flops 2417885184 | bytes 9437184 | tf_op jit(solution)/shard_map/dot_general | solution.py:48
  123.4 3.1 %all-to-all-done.4 = bf16[32,24,128]{2,1,0:T(8,128)(2,1)S(1)} async-done(((bf16[32,24,128]{2,1,0:T(8,128)(2,1)}), bf16[32,24,128]{2,1,0:T(8,128)(2,1)S(1)}, u32[]{:S(2)}, u32[]{:S(2)}) %all-to-all-start.4) | async-done | bytes 196640 | tf_op jit(solution)/shard_map/all_to_all | solution.py:19
  126.4 6.9 %all-to-all-start.5 = ((bf16[32,16,1536]{2,1,0:T(8,128)(2,1)}), bf16[32,16,1536]{2,1,0:T(8,128)(2,1)S(1)}, u32[]{:S(2)}, u32[]{:S(2)}) async-start(bf16[32,16,1536]{2,1,0:T(8,128)(2,1)} %bitcast.20), calls=%async_computation.5 | async-start | bytes 3145728 | tf_op jit(solution)/shard_map/all_to_all | solution.py:19
  133.5 0.2 slice_reduce_fusion.1
  133.7 0.1 convolution_convert_fusion.7
  133.9 20.2 %all_gather.15 = bf16[512,48]{1,0:T(8,128)(2,1)S(1)} all-gather(bf16[32,48]{1,0:T(8,128)(2,1)S(1)} %convolution_convert_fusion.7), channel_id=1, replica_groups=mesh['dp'=16,'y'=8,'x'=4] {'dp'}, dimensions={0}, use_global_device_ids=true | all-gather | bytes 52224 | tf_op jit(solution)/shard_map/all_gather | solution.py:176
  154.0 0.2 convolution_convert_fusion.6
  154.2 15.4 %all-to-all-done.5 = bf16[32,16,1536]{2,1,0:T(8,128)(2,1)S(1)} async-done(((bf16[32,16,1536]{2,1,0:T(8,128)(2,1)}), bf16[32,16,1536]{2,1,0:T(8,128)(2,1)S(1)}, u32[]{:S(2)}, u32[]{:S(2)}) %all-to-all-start.5) | async-done | bytes 1572896 | tf_op jit(solution)/shard_map/all_to_all | solution.py:19
  169.7 0.7 broadcast_in_dim.151
  170.4 6.5 %all-to-all-start.6 = ((bf16[32,12,128]{2,1,0:T(8,128)(2,1)}), bf16[32,12,128]{2,1,0:T(8,128)(2,1)S(1)}, u32[]{:S(2)}, u32[]{:S(2)}) async-start(bf16[32,12,128]{2,1,0:T(8,128)(2,1)} %broadcast_in_dim.151), calls=%async_computation.6 | async-start | bytes 262144 | tf_op jit(solution)/shard_map/all_to_all | solution.py:19
  176.9 0.4 convolution_bitcast_fusion.2
  177.3 0.4 fusion.2
  177.8 8.7 %all-to-all-done.6 = bf16[32,12,128]{2,1,0:T(8,128)(2,1)S(1)} async-done(((bf16[32,12,128]{2,1,0:T(8,128)(2,1)}), bf16[32,12,128]{2,1,0:T(8,128)(2,1)S(1)}, u32[]{:S(2)}, u32[]{:S(2)}) %all-to-all-start.6) | async-done | bytes 98336 | tf_op jit(solution)/shard_map/all_to_all | solution.py:19
  186.4 0.2 reshape.243
  186.8 0.3 reshape.244
  187.1 0.2 fusion.33
  187.4 2.4 %fusion.10 = f32[32,768]{1,0:T(8,128)S(1)} fusion(bf16[3,768,1536]{2,1,0:T(8,128)(2,1)} %all-gather.4.cloned.1.call-done, bf16[32,1536]{1,0:T(8,128)(2,1)S(1)} %get-tuple-element.35, f32[1536]{0:T(1024)S(1)} %copy-done.5, f32[32]{0:T(128)S(1)} %add_rsqrt_fusion), kind=kOutput, calls=%fused_computation.23 | convolution fusion | flops 75718656 | bytes 2562176 | tf_op jit(solution)/shard_map/dot_general | solution.py:13
  189.8 3.9 %convolution_convert_fusion.2 = bf16[32,1536]{1,0:T(8,128)(2,1)S(1)} fusion(bf16[3,768,1536]{2,1,0:T(8,128)(2,1)} %all-gather.4.cloned.1.call-done, f32[32,768]{1,0:T(8,128)S(1)} %fusion.10, bf16[32,1536]{1,0:T(8,128)(2,1)S(1)} %get-tuple-element.35, f32[1536]{0:T(1024)S(1)} %copy-done.5, f32[32]{0:T(128)S(1)} %add_rsqrt_fusion), kind=kOutput, calls=%fused_computation.12 | convolution fusion | flops 151289856 | bytes 5019776 | tf_op jit(solution)/shard_map/dot_general | solution.py:48
  193.8 0.8 reshape.245
  194.5 4.7 %all-to-all-start.7 = ((bf16[32,12,128]{2,1,0:T(8,128)(2,1)}), bf16[32,12,128]{2,1,0:T(8,128)(2,1)S(1)}, u32[]{:S(2)}, u32[]{:S(2)}) async-start(bf16[32,12,128]{2,1,0:T(8,128)(2,1)} %reshape.245), calls=%async_computation.7 | async-start | bytes 262144 | tf_op jit(solution)/shard_map/all_to_all | solution.py:19
  199.2 1.1 fusion.3
  200.3 8.5 %all-to-all-done.7 = bf16[32,12,128]{2,1,0:T(8,128)(2,1)S(1)} async-done(((bf16[32,12,128]{2,1,0:T(8,128)(2,1)}), bf16[32,12,128]{2,1,0:T(8,128)(2,1)S(1)}, u32[]{:S(2)}, u32[]{:S(2)}) %all-to-all-start.7) | async-done | bytes 98336 | tf_op jit(solution)/shard_map/all_to_all | solution.py:19
  208.9 0.6 fusion.74
  (93 shorter events, 2.5 us)
Async XLA Ops:
  7.2 126.5 %copy-start = (bf16[1536,48]{0,1:T(8,128)(2,1)S(1)}, bf16[1536,48]{0,1:T(8,128)(2,1)}, u32[]{:S(2)}) copy-start(bf16[1536,48]{0,1:T(8,128)(2,1)} %param.24) | copy-start | bytes 442372
  7.2 5.2 %copy-start.4 = (bf16[1,48,1536]{2,1,0:T(8,128)(2,1)S(1)}, bf16[1,48,1536]{2,1,0:T(8,128)(2,1)}, u32[]{:S(2)}) copy-start(bf16[1,48,1536]{2,1,0:T(8,128)(2,1)} %param.29) | copy-start | bytes 442372
  7.2 5.2 %copy-start.3 = (bf16[1,48,1536]{2,1,0:T(8,128)(2,1)S(1)}, bf16[1,48,1536]{2,1,0:T(8,128)(2,1)}, u32[]{:S(2)}) copy-start(bf16[1,48,1536]{2,1,0:T(8,128)(2,1)} %param.30) | copy-start | bytes 442372
  7.2 5.2 %copy-start.2 = (bf16[1,48,1536]{2,1,0:T(8,128)(2,1)S(1)}, bf16[1,48,1536]{2,1,0:T(8,128)(2,1)}, u32[]{:S(2)}) copy-start(bf16[1,48,1536]{2,1,0:T(8,128)(2,1)} %param.31) | copy-start | bytes 442372
  7.2 93.4 %all-gather.4.cloned.1.call-start = ((), (), s32[]{:S(2)}) async-start(), calls=%async_computation.8 | async-start | bytes 7520256 | tf_op jit(solution)/shard_map/all_gather | solution.py:105
  10.6 2.7 %copy-start.8 = (bf16[1,1536]{1,0:T(2,128)(2,1)S(1)}, bf16[1,1536]{1,0:T(2,128)(2,1)}, u32[]{:S(2)}) copy-start(bf16[1,1536]{1,0:T(2,128)(2,1)} %param.16) | copy-start | bytes 9220
  10.6 2.7 %copy-start.10 = (bf16[1,512]{1,0:T(2,128)(2,1)S(1)}, bf16[1,512]{1,0:T(2,128)(2,1)}, u32[]{:S(2)}) copy-start(bf16[1,512]{1,0:T(2,128)(2,1)} %param.17) | copy-start | bytes 3076
  13.3 46.1 %copy-start.14 = (s32[512]{0:T(512)S(1)}, s32[512]{0:T(512)}, u32[]{:S(2)}) copy-start(s32[512]{0:T(512)} %param.19) | copy-start | bytes 6148
  13.3 48.6 %all-to-all-start = ((bf16[32,16,1536]{2,1,0:T(8,128)(2,1)}), bf16[32,16,1536]{2,1,0:T(8,128)(2,1)S(1)}, u32[]{:S(2)}, u32[]{:S(2)}) async-start(bf16[32,16,1536]{2,1,0:T(8,128)(2,1)} %bitcast.3), calls=%async_computation | async-start | bytes 3145728 | tf_op jit(solution)/shard_map/all_to_all | solution.py:19
  23.5 61.5 %copy-start.11 = (s32[32]{0:T(128)S(1)}, s32[32]{0:T(128)}, u32[]{:S(2)}) copy-start(s32[32]{0:T(128)} %param.20) | copy-start | bytes 388
  23.5 61.5 %copy-start.12 = (s32[32]{0:T(128)S(1)}, s32[32]{0:T(128)}, u32[]{:S(2)}) copy-start(s32[32]{0:T(128)} %param.21) | copy-start | bytes 388
  23.5 61.7 %copy-start.9 = (bf16[1,1536]{1,0:T(2,128)(2,1)S(1)}, bf16[1,1536]{1,0:T(2,128)(2,1)}, u32[]{:S(2)}) copy-start(bf16[1,1536]{1,0:T(2,128)(2,1)} %param.18) | copy-start | bytes 9220
  23.6 67.5 %copy-start.13 = (bf16[32,2,64,128]{3,2,1,0:T(8,128)(2,1)S(1)}, bf16[32,2,64,128]{3,2,1,0:T(8,128)(2,1)}, u32[]{:S(2)}) copy-start(bf16[32,2,64,128]{3,2,1,0:T(8,128)(2,1)} %param.22) | copy-start | bytes 3145732
  61.9 18.9 %all-to-all-start.1 = ((bf16[8,32,512]{2,1,0:T(8,128)(2,1)}), bf16[8,32,512]{2,1,0:T(8,128)(2,1)S(1)}, u32[]{:S(2)}, u32[]{:S(2)}) async-start(bf16[8,32,512]{2,1,0:T(8,128)(2,1)} %bitcast.4), calls=%async_computation.1 | async-start | bytes 524288 | tf_op jit(solution)/shard_map/all_to_all | solution.py:19
  81.7 9.3 %all-to-all-start.2 = ((bf16[4,32,512]{2,1,0:T(8,128)(2,1)}), bf16[4,32,512]{2,1,0:T(8,128)(2,1)S(1)}, u32[]{:S(2)}, u32[]{:S(2)}) async-start(bf16[4,32,512]{2,1,0:T(8,128)(2,1)} %bitcast.6), calls=%async_computation.2 | async-start | bytes 262144 | tf_op jit(solution)/shard_map/all_to_all | solution.py:19
  95.6 14.6 %all-to-all-start.3 = ((bf16[32,16,128]{2,1,0:T(8,128)(2,1)}), bf16[32,16,128]{2,1,0:T(8,128)(2,1)S(1)}, u32[]{:S(2)}, u32[]{:S(2)}) async-start(bf16[32,16,128]{2,1,0:T(8,128)(2,1)} %copy.83), calls=%async_computation.3 | async-start | bytes 262144 | tf_op jit(solution)/shard_map/all_to_all | solution.py:19
  111.4 15.0 %all-to-all-start.4 = ((bf16[32,24,128]{2,1,0:T(8,128)(2,1)}), bf16[32,24,128]{2,1,0:T(8,128)(2,1)S(1)}, u32[]{:S(2)}, u32[]{:S(2)}) async-start(bf16[32,24,128]{2,1,0:T(8,128)(2,1)} %broadcast_in_dim.147), calls=%async_computation.4 | async-start | bytes 393216 | tf_op jit(solution)/shard_map/all_to_all | solution.py:19
  126.4 7.0 %copy-start.7 = (f32[64,4]{0,1:T(4,128)S(1)}, f32[64,4]{0,1:T(4,128)}, u32[]{:S(2)}) copy-start(f32[64,4]{0,1:T(4,128)} %param.27) | copy-start | bytes 3076
  126.4 7.0 %copy-start.6 = (s32[64,4]{0,1:T(4,128)S(1)}, s32[64,4]{0,1:T(4,128)}, u32[]{:S(2)}) copy-start(s32[64,4]{0,1:T(4,128)} %param.26) | copy-start | bytes 3076
  126.4 43.2 %all-to-all-start.5 = ((bf16[32,16,1536]{2,1,0:T(8,128)(2,1)}), bf16[32,16,1536]{2,1,0:T(8,128)(2,1)S(1)}, u32[]{:S(2)}, u32[]{:S(2)}) async-start(bf16[32,16,1536]{2,1,0:T(8,128)(2,1)} %bitcast.20), calls=%async_computation.5 | async-start | bytes 3145728 | tf_op jit(solution)/shard_map/all_to_all | solution.py:19
  170.4 16.0 %all-to-all-start.6 = ((bf16[32,12,128]{2,1,0:T(8,128)(2,1)}), bf16[32,12,128]{2,1,0:T(8,128)(2,1)S(1)}, u32[]{:S(2)}, u32[]{:S(2)}) async-start(bf16[32,12,128]{2,1,0:T(8,128)(2,1)} %broadcast_in_dim.151), calls=%async_computation.6 | async-start | bytes 262144 | tf_op jit(solution)/shard_map/all_to_all | solution.py:19
  177.3 10.0 %copy-start.5 = (f32[1536]{0:T(1024)S(1)}, f32[1536]{0:T(1024)}, u32[]{:S(2)}) copy-start(f32[1536]{0:T(1024)} %param.28) | copy-start | bytes 18436
  189.8 9.4 %copy-start.1 = (bf16[63,1536]{1,0:T(8,128)(2,1)S(1)}, bf16[63,1536]{1,0:T(8,128)(2,1)}, u32[]{:S(2)}) copy-start(bf16[63,1536]{1,0:T(8,128)(2,1)} %param.25) | copy-start | bytes 580612
  194.5 14.3 %all-to-all-start.7 = ((bf16[32,12,128]{2,1,0:T(8,128)(2,1)}), bf16[32,12,128]{2,1,0:T(8,128)(2,1)S(1)}, u32[]{:S(2)}, u32[]{:S(2)}) async-start(bf16[32,12,128]{2,1,0:T(8,128)(2,1)} %reshape.245), calls=%async_computation.7 | async-start | bytes 262144 | tf_op jit(solution)/shard_map/all_to_all | solution.py:19
Sparse Core Ops, SparseCore 0:
  13.4 58.0 all-gather.3
where the time goes:
time: 217 us; the launch traced here: 216 us
  waiting for transfers between devices  58.8 us (27%)
  blocking collectives  56 us (26%)
  starting transfers between devices  49.3 us (23%)
  matrix products  26.8 us (12%)
  between operations  14.6 us (7%)
  other arithmetic  6.01 us (3%)
  local copies, waits for them, and re-layouts  4.88 us (2%)
    all_to_all x8, waiting for transfers between devices, swap(): lax.all_to_all(blocks, axis_name, split_axis=0, concat_axis=0, tiled=True)  58.7 us
    all_to_all x8, starting transfers between devices, swap(): lax.all_to_all(blocks, axis_name, split_axis=0, concat_axis=0, tiled=True)  49.3 us
    all_gather x1, blocking collectives, on_device(): all_rows = lax.all_gather(line_share, 'dp', axis=0, tiled=True)  23.4 us
    all_gather x1, blocking collectives, on_device(): all_projected = lax.all_gather(projected, 'dp', axis=0, tiled=True)  20.2 us
    all_gather x1, blocking collectives, on_device(): line_fresh = lax.all_gather(fresh, 'x', axis=0, tiled=True)  12.4 us
    dot_general x2, matrix products, expert_units(): return jnp.dot(active, units[2], preferred_element_type=F32).astype(BF16)  11.1 us
    dot_general x2, matrix products, contract_rows(): lax.dot_general(left_rows, unit_rows, (((1,), (1,)), ((), ())), preferred...  6.75 us
  transfers between devices with their start and end apart: 9, of which 8 were waited for; matrix products, arithmetic and copies ran while one was open for 10% of the time, Pallas kernels for 0%

commit v1 on v0

--- a/solution.py
+++ b/solution.py
@@ -3,6 +3,7 @@
 from jax import lax
 from jax.sharding import Mesh
 from jax.sharding import PartitionSpec as P
+from jax.lax import all_to_all, axis_size
 
 TP = ("y", "x")
 F32 = jnp.float32
@@ -173,7 +174,9 @@
     attention = group_rows[:, :heads].reshape(group_reqs, width)
     resid_rows = group_rows[:, heads:].reshape(group_reqs, width)
     projected = jnp.dot(attention, w_out, preferred_element_type=F32).astype(BF16)
-    all_projected = lax.all_gather(projected, "dp", axis=0, tiled=True)
+    all_projected = jnp.concatenate(
+        all_to_all(jnp.stack([projected] * axis_size("dp")), "dp", 0, 0), 0
+    )
     home_ids = dp_group * group_reqs + jnp.arange(group_reqs, dtype=jnp.int32)
     at_home = choose_rows(home_ids[:, None] == placing[None, :], all_projected)
     at_home, returned = lax.optimization_barrier((at_home, returned))

time: 217 us -> 235 us (1.083)
  waiting for transfers between devices: 58.8 us -> 81.4 us
  blocking collectives: 56 us -> 50.4 us
    all_to_all x8, waiting for transfers between devices: 58.7 us -> 81.4 us  [swap(): lax.all_to_all(blocks, axis_name, split_axis=0, concat_axis=0, tiled=True)]
    all_gather x1 -> x0, blocking collectives: 20.2 us -> none  [on_device(): all_projected = lax.all_gather(projected, 'dp', axis=0, tiled=True)]
    all_to_all x0 -> x1, blocking collectives: none -> 14.6 us  [on_device(): all_to_all(jnp.stack([projected] * axis_size('dp')), 'dp', 0, 0)]
  transfers between devices with their start and end apart: 9 -> 9, of which waited for: 8 -> 8; matrix products, arithmetic and copies ran while one was open for 10% -> 9% of each run, Pallas kernels for 0% -> 0%
where the time goes in v1:
time: 235 us; the launch traced here: 234 us
  waiting for transfers between devices  81.4 us (35%)
  blocking collectives  50.4 us (21%)
  starting transfers between devices  49.5 us (21%)
  matrix products  26.8 us (11%)
  between operations  14.6 us (6%)
  other arithmetic  6.02 us (3%)
  local copies, waits for them, and re-layouts  5.26 us (2%)
    all_to_all x8, waiting for transfers between devices, swap(): lax.all_to_all(blocks, axis_name, split_axis=0, concat_axis=0, tiled=True)  81.4 us
    all_to_all x8, starting transfers between devices, swap(): lax.all_to_all(blocks, axis_name, split_axis=0, concat_axis=0, tiled=True)  49.5 us
    all_gather x1, blocking collectives, on_device(): all_rows = lax.all_gather(line_share, 'dp', axis=0, tiled=True)  23.4 us
    all_to_all x1, blocking collectives, on_device(): all_to_all(jnp.stack([projected] * axis_size('dp')), 'dp', 0, 0)  14.6 us
    all_gather x1, blocking collectives, on_device(): line_fresh = lax.all_gather(fresh, 'x', axis=0, tiled=True)  12.4 us
    dot_general x2, matrix products, expert_units(): return jnp.dot(active, units[2], preferred_element_type=F32).astype(BF16)  11.1 us
    dot_general x2, matrix products, contract_rows(): lax.dot_general(left_rows, unit_rows, (((1,), (1,)), ((), ())), preferred...  6.75 us
  transfers between devices with their start and end apart: 9, of which 8 were waited for; matrix products, arithmetic and copies ran while one was open for 9% of the time, Pallas kernels for 0%

profile of v1, /device:TPU:8, one launch (start us, length us, event | category | flops | bytes accessed | tf_op | source)
XLA Modules:
  0.0 234.0 jit_solution(11913844897924331075)
XLA Ops:
  7.3 0.8 iota_compare_fusion.1
  8.3 1.1 fusion.20
  9.4 1.1 fusion.22
  10.6 1.8 convolution_convert_fusion.1
  12.4 0.8 pad_maximum_fusion
  13.3 10.2 %all-to-all-start = ((bf16[32,16,1536]{2,1,0:T(8,128)(2,1)}), bf16[32,16,1536]{2,1,0:T(8,128)(2,1)S(1)}, u32[]{:S(2)}, u32[]{:S(2)}) async-start(bf16[32,16,1536]{2,1,0:T(8,128)(2,1)} %bitcast.3), calls=%async_computation | async-start | bytes 3145728 | tf_op jit(solution)/shard_map/all_to_all | solution.py:20
  23.6 12.4 %all-gather = bf16[4,1,2048]{2,1,0:T(2,128)(2,1)S(1)} all-gather(bf16[1,1,2048]{2,1,0:T(2,128)(2,1)S(1)} %bitcast.121), channel_id=1, replica_groups=mesh['dp'=16,'y'=8,'x'=4] {'x'}, dimensions={0}, use_global_device_ids=true | all-gather | bytes 20480 | tf_op jit(solution)/shard_map/all_gather | solution.py:113
  36.0 23.4 %all-gather.1 = bf16[16,4,512]{2,1,0:T(4,128)(2,1)S(1)} all-gather(bf16[1,4,512]{2,1,0:T(4,128)(2,1)S(1)} %bitcast.123), channel_id=1, replica_groups=mesh['dp'=16,'y'=8,'x'=4] {'dp'}, dimensions={0}, use_global_device_ids=true | all-gather | bytes 69632 | tf_op jit(solution)/shard_map/all_gather | solution.py:115
  59.8 1.0 convolution_convert_fusion.3
  60.8 1.2 all-to-all-done
  61.9 8.0 %all-to-all-start.1 = ((bf16[8,32,512]{2,1,0:T(8,128)(2,1)}), bf16[8,32,512]{2,1,0:T(8,128)(2,1)S(1)}, u32[]{:S(2)}, u32[]{:S(2)}) async-start(bf16[8,32,512]{2,1,0:T(8,128)(2,1)} %bitcast.4), calls=%async_computation.1 | async-start | bytes 524288 | tf_op jit(solution)/shard_map/all_to_all | solution.py:20
  69.9 10.9 %all-to-all-done.1 = bf16[8,32,512]{2,1,0:T(8,128)(2,1)S(1)} async-done(((bf16[8,32,512]{2,1,0:T(8,128)(2,1)}), bf16[8,32,512]{2,1,0:T(8,128)(2,1)S(1)}, u32[]{:S(2)}, u32[]{:S(2)}) %all-to-all-start.1) | async-done | bytes 262176 | tf_op jit(solution)/shard_map/all_to_all | solution.py:20
  80.8 0.9 convolution_convert_fusion.4
  81.7 3.3 %all-to-all-start.2 = ((bf16[4,32,512]{2,1,0:T(8,128)(2,1)}), bf16[4,32,512]{2,1,0:T(8,128)(2,1)S(1)}, u32[]{:S(2)}, u32[]{:S(2)}) async-start(bf16[4,32,512]{2,1,0:T(8,128)(2,1)} %bitcast.6), calls=%async_computation.2 | async-start | bytes 262144 | tf_op jit(solution)/shard_map/all_to_all | solution.py:20
  85.3 5.7 %all-to-all-done.2 = bf16[4,32,512]{2,1,0:T(8,128)(2,1)S(1)} async-done(((bf16[4,32,512]{2,1,0:T(8,128)(2,1)}), bf16[4,32,512]{2,1,0:T(8,128)(2,1)S(1)}, u32[]{:S(2)}, u32[]{:S(2)}) %all-to-all-start.2) | async-done | bytes 131104 | tf_op jit(solution)/shard_map/all_to_all | solution.py:20
  91.1 1.1 fusion.83
  92.3 0.3 reduce-precision_convert_fusion
  92.6 1.7 fusion.12
  94.9 0.7 copy.83
  95.6 5.0 %all-to-all-start.3 = ((bf16[32,16,128]{2,1,0:T(8,128)(2,1)}), bf16[32,16,128]{2,1,0:T(8,128)(2,1)S(1)}, u32[]{:S(2)}, u32[]{:S(2)}) async-start(bf16[32,16,128]{2,1,0:T(8,128)(2,1)} %copy.83), calls=%async_computation.3 | async-start | bytes 262144 | tf_op jit(solution)/shard_map/all_to_all | solution.py:20
  100.6 4.3 %fusion.5 = f32[512,768]{1,0:T(8,128)} fusion(bf16[512,1536]{1,0:T(8,128)(2,1)S(1)} %bitcast.107, bf16[3,768,1536]{2,1,0:T(8,128)(2,1)} %all-gather.4.cloned.1.call-done), kind=kOutput, calls=%fused_computation.14 | convolution fusion | flops 1207959552 | bytes 5505024 | tf_op jit(solution)/shard_map/dot_general | solution.py:14
  104.9 5.3 %all-to-all-done.3 = bf16[32,16,128]{2,1,0:T(8,128)(2,1)S(1)} async-done(((bf16[32,16,128]{2,1,0:T(8,128)(2,1)}), bf16[32,16,128]{2,1,0:T(8,128)(2,1)S(1)}, u32[]{:S(2)}, u32[]{:S(2)}) %all-to-all-start.3) | async-done | bytes 131104 | tf_op jit(solution)/shard_map/all_to_all | solution.py:20
  110.7 0.7 broadcast_in_dim.147
  111.4 4.7 %all-to-all-start.4 = ((bf16[32,24,128]{2,1,0:T(8,128)(2,1)}), bf16[32,24,128]{2,1,0:T(8,128)(2,1)S(1)}, u32[]{:S(2)}, u32[]{:S(2)}) async-start(bf16[32,24,128]{2,1,0:T(8,128)(2,1)} %broadcast_in_dim.147), calls=%async_computation.4 | async-start | bytes 393216 | tf_op jit(solution)/shard_map/all_to_all | solution.py:20
  116.1 7.2 %convolution_convert_fusion = bf16[512,1536]{1,0:T(8,128)(2,1)} fusion(bf16[3,768,1536]{2,1,0:T(8,128)(2,1)} %all-gather.4.cloned.1.call-done, f32[512,768]{1,0:T(8,128)} %fusion.5, bf16[512,1536]{1,0:T(8,128)(2,1)S(1)} %bitcast.108), kind=kOutput, calls=%fused_computation | convolution fusion | flops 2417885184 | bytes 9437184 | tf_op jit(solution)/shard_map/dot_general | solution.py:49
  123.4 3.1 %all-to-all-done.4 = bf16[32,24,128]{2,1,0:T(8,128)(2,1)S(1)} async-done(((bf16[32,24,128]{2,1,0:T(8,128)(2,1)}), bf16[32,24,128]{2,1,0:T(8,128)(2,1)S(1)}, u32[]{:S(2)}, u32[]{:S(2)}) %all-to-all-start.4) | async-done | bytes 196640 | tf_op jit(solution)/shard_map/all_to_all | solution.py:20
  126.7 0.2 reshape.265
  126.9 14.6 %all_to_all.45 = bf16[16,2,768]{2,1,0:T(2,128)(2,1)S(1)} all-to-all(bf16[16,2,768]{2,1,0:T(2,128)(2,1)S(1)} %reshape.265), channel_id=1, replica_groups=mesh['dp'=16,'y'=8,'x'=4] {'dp'}, dimensions={0} | all-to-all | bytes 98304 | tf_op jit(solution)/shard_map/all_to_all | solution.py:178
  141.4 7.0 %all-to-all-start.6 = ((bf16[32,16,1536]{2,1,0:T(8,128)(2,1)}), bf16[32,16,1536]{2,1,0:T(8,128)(2,1)S(1)}, u32[]{:S(2)}, u32[]{:S(2)}) async-start(bf16[32,16,1536]{2,1,0:T(8,128)(2,1)} %bitcast.21), calls=%async_computation.6 | async-start | bytes 3145728 | tf_op jit(solution)/shard_map/all_to_all | solution.py:20
  148.5 0.2 slice_reduce_fusion.1
  148.7 0.2 reshape.266
  148.9 0.2 convolution_convert_fusion.6
  149.0 38.1 %all-to-all-done.6 = bf16[32,16,1536]{2,1,0:T(8,128)(2,1)S(1)} async-done(((bf16[32,16,1536]{2,1,0:T(8,128)(2,1)}), bf16[32,16,1536]{2,1,0:T(8,128)(2,1)S(1)}, u32[]{:S(2)}, u32[]{:S(2)}) %all-to-all-start.6) | async-done | bytes 1572896 | tf_op jit(solution)/shard_map/all_to_all | solution.py:20
  187.2 0.7 broadcast_in_dim.151
  187.9 6.5 %all-to-all-start.7 = ((bf16[32,12,128]{2,1,0:T(8,128)(2,1)}), bf16[32,12,128]{2,1,0:T(8,128)(2,1)S(1)}, u32[]{:S(2)}, u32[]{:S(2)}) async-start(bf16[32,12,128]{2,1,0:T(8,128)(2,1)} %broadcast_in_dim.151), calls=%async_computation.7 | async-start | bytes 262144 | tf_op jit(solution)/shard_map/all_to_all | solution.py:20
  194.4 0.4 convolution_bitcast_fusion.2
  194.8 0.4 fusion.2
  195.3 8.7 %all-to-all-done.7 = bf16[32,12,128]{2,1,0:T(8,128)(2,1)S(1)} async-done(((bf16[32,12,128]{2,1,0:T(8,128)(2,1)}), bf16[32,12,128]{2,1,0:T(8,128)(2,1)S(1)}, u32[]{:S(2)}, u32[]{:S(2)}) %all-to-all-start.7) | async-done | bytes 98336 | tf_op jit(solution)/shard_map/all_to_all | solution.py:20
  203.9 0.2 reshape.249
  204.3 0.3 reshape.250
  204.6 0.2 fusion.33
  204.8 2.4 %fusion.10 = f32[32,768]{1,0:T(8,128)S(1)} fusion(bf16[3,768,1536]{2,1,0:T(8,128)(2,1)} %all-gather.4.cloned.1.call-done, bf16[32,1536]{1,0:T(8,128)(2,1)S(1)} %get-tuple-element.35, f32[1536]{0:T(1024)S(1)} %copy-done.5, f32[32]{0:T(128)S(1)} %add_rsqrt_fusion), kind=kOutput, calls=%fused_computation.23 | convolution fusion | flops 75718656 | bytes 2562176 | tf_op jit(solution)/shard_map/dot_general | solution.py:14
  207.3 3.9 %convolution_convert_fusion.2 = bf16[32,1536]{1,0:T(8,128)(2,1)S(1)} fusion(bf16[3,768,1536]{2,1,0:T(8,128)(2,1)} %all-gather.4.cloned.1.call-done, f32[32,768]{1,0:T(8,128)S(1)} %fusion.10, bf16[32,1536]{1,0:T(8,128)(2,1)S(1)} %get-tuple-element.35, f32[1536]{0:T(1024)S(1)} %copy-done.5, f32[32]{0:T(128)S(1)} %add_rsqrt_fusion), kind=kOutput, calls=%fused_computation.12 | convolution fusion | flops 151289856 | bytes 5019776 | tf_op jit(solution)/shard_map/dot_general | solution.py:49
  211.2 0.8 reshape.251
  212.0 4.8 %all-to-all-start.8 = ((bf16[32,12,128]{2,1,0:T(8,128)(2,1)}), bf16[32,12,128]{2,1,0:T(8,128)(2,1)S(1)}, u32[]{:S(2)}, u32[]{:S(2)}) async-start(bf16[32,12,128]{2,1,0:T(8,128)(2,1)} %reshape.251), calls=%async_computation.8 | async-start | bytes 262144 | tf_op jit(solution)/shard_map/all_to_all | solution.py:20
  216.8 1.1 fusion.3
  218.0 8.5 %all-to-all-done.8 = bf16[32,12,128]{2,1,0:T(8,128)(2,1)S(1)} async-done(((bf16[32,12,128]{2,1,0:T(8,128)(2,1)}), bf16[32,12,128]{2,1,0:T(8,128)(2,1)S(1)}, u32[]{:S(2)}, u32[]{:S(2)}) %all-to-all-start.8) | async-done | bytes 98336 | tf_op jit(solution)/shard_map/all_to_all | solution.py:20
  226.6 0.6 fusion.74
  (96 shorter events, 2.8 us)
Async XLA Ops:
  7.2 119.3 %copy-start = (bf16[1536,48]{0,1:T(8,128)(2,1)S(1)}, bf16[1536,48]{0,1:T(8,128)(2,1)}, u32[]{:S(2)}) copy-start(bf16[1536,48]{0,1:T(8,128)(2,1)} %param.24) | copy-start | bytes 442372
  7.2 5.2 %copy-start.4 = (bf16[1,48,1536]{2,1,0:T(8,128)(2,1)S(1)}, bf16[1,48,1536]{2,1,0:T(8,128)(2,1)}, u32[]{:S(2)}) copy-start(bf16[1,48,1536]{2,1,0:T(8,128)(2,1)} %param.29) | copy-start | bytes 442372
  7.2 5.2 %copy-start.3 = (bf16[1,48,1536]{2,1,0:T(8,128)(2,1)S(1)}, bf16[1,48,1536]{2,1,0:T(8,128)(2,1)}, u32[]{:S(2)}) copy-start(bf16[1,48,1536]{2,1,0:T(8,128)(2,1)} %param.30) | copy-start | bytes 442372
  7.2 5.2 %copy-start.2 = (bf16[1,48,1536]{2,1,0:T(8,128)(2,1)S(1)}, bf16[1,48,1536]{2,1,0:T(8,128)(2,1)}, u32[]{:S(2)}) copy-start(bf16[1,48,1536]{2,1,0:T(8,128)(2,1)} %param.31) | copy-start | bytes 442372
  7.2 93.4 %all-gather.4.cloned.1.call-start = ((), (), s32[]{:S(2)}) async-start(), calls=%async_computation.9 | async-start | bytes 7520256 | tf_op jit(solution)/shard_map/all_gather | solution.py:106
  10.6 2.7 %copy-start.8 = (bf16[1,1536]{1,0:T(2,128)(2,1)S(1)}, bf16[1,1536]{1,0:T(2,128)(2,1)}, u32[]{:S(2)}) copy-start(bf16[1,1536]{1,0:T(2,128)(2,1)} %param.16) | copy-start | bytes 9220
  10.6 2.7 %copy-start.10 = (bf16[1,512]{1,0:T(2,128)(2,1)S(1)}, bf16[1,512]{1,0:T(2,128)(2,1)}, u32[]{:S(2)}) copy-start(bf16[1,512]{1,0:T(2,128)(2,1)} %param.17) | copy-start | bytes 3076
  13.3 46.1 %copy-start.14 = (s32[512]{0:T(512)S(1)}, s32[512]{0:T(512)}, u32[]{:S(2)}) copy-start(s32[512]{0:T(512)} %param.19) | copy-start | bytes 6148
  13.3 48.6 %all-to-all-start = ((bf16[32,16,1536]{2,1,0:T(8,128)(2,1)}), bf16[32,16,1536]{2,1,0:T(8,128)(2,1)S(1)}, u32[]{:S(2)}, u32[]{:S(2)}) async-start(bf16[32,16,1536]{2,1,0:T(8,128)(2,1)} %bitcast.3), calls=%async_computation | async-start | bytes 3145728 | tf_op jit(solution)/shard_map/all_to_all | solution.py:20
  23.5 61.5 %copy-start.11 = (s32[32]{0:T(128)S(1)}, s32[32]{0:T(128)}, u32[]{:S(2)}) copy-start(s32[32]{0:T(128)} %param.20) | copy-start | bytes 388
  23.5 61.5 %copy-start.12 = (s32[32]{0:T(128)S(1)}, s32[32]{0:T(128)}, u32[]{:S(2)}) copy-start(s32[32]{0:T(128)} %param.21) | copy-start | bytes 388
  23.5 61.7 %copy-start.9 = (bf16[1,1536]{1,0:T(2,128)(2,1)S(1)}, bf16[1,1536]{1,0:T(2,128)(2,1)}, u32[]{:S(2)}) copy-start(bf16[1,1536]{1,0:T(2,128)(2,1)} %param.18) | copy-start | bytes 9220
  23.6 67.5 %copy-start.13 = (bf16[32,2,64,128]{3,2,1,0:T(8,128)(2,1)S(1)}, bf16[32,2,64,128]{3,2,1,0:T(8,128)(2,1)}, u32[]{:S(2)}) copy-start(bf16[32,2,64,128]{3,2,1,0:T(8,128)(2,1)} %param.22) | copy-start | bytes 3145732
  61.9 18.9 %all-to-all-start.1 = ((bf16[8,32,512]{2,1,0:T(8,128)(2,1)}), bf16[8,32,512]{2,1,0:T(8,128)(2,1)S(1)}, u32[]{:S(2)}, u32[]{:S(2)}) async-start(bf16[8,32,512]{2,1,0:T(8,128)(2,1)} %bitcast.4), calls=%async_computation.1 | async-start | bytes 524288 | tf_op jit(solution)/shard_map/all_to_all | solution.py:20
  81.7 9.3 %all-to-all-start.2 = ((bf16[4,32,512]{2,1,0:T(8,128)(2,1)}), bf16[4,32,512]{2,1,0:T(8,128)(2,1)S(1)}, u32[]{:S(2)}, u32[]{:S(2)}) async-start(bf16[4,32,512]{2,1,0:T(8,128)(2,1)} %bitcast.6), calls=%async_computation.2 | async-start | bytes 262144 | tf_op jit(solution)/shard_map/all_to_all | solution.py:20
  95.6 14.6 %all-to-all-start.3 = ((bf16[32,16,128]{2,1,0:T(8,128)(2,1)}), bf16[32,16,128]{2,1,0:T(8,128)(2,1)S(1)}, u32[]{:S(2)}, u32[]{:S(2)}) async-start(bf16[32,16,128]{2,1,0:T(8,128)(2,1)} %copy.83), calls=%async_computation.3 | async-start | bytes 262144 | tf_op jit(solution)/shard_map/all_to_all | solution.py:20
  111.4 15.0 %all-to-all-start.4 = ((bf16[32,24,128]{2,1,0:T(8,128)(2,1)}), bf16[32,24,128]{2,1,0:T(8,128)(2,1)S(1)}, u32[]{:S(2)}, u32[]{:S(2)}) async-start(bf16[32,24,128]{2,1,0:T(8,128)(2,1)} %broadcast_in_dim.147), calls=%async_computation.4 | async-start | bytes 393216 | tf_op jit(solution)/shard_map/all_to_all | solution.py:20
  141.4 7.0 %copy-start.7 = (f32[64,4]{0,1:T(4,128)S(1)}, f32[64,4]{0,1:T(4,128)}, u32[]{:S(2)}) copy-start(f32[64,4]{0,1:T(4,128)} %param.27) | copy-start | bytes 3076
  141.4 7.0 %copy-start.6 = (s32[64,4]{0,1:T(4,128)S(1)}, s32[64,4]{0,1:T(4,128)}, u32[]{:S(2)}) copy-start(s32[64,4]{0,1:T(4,128)} %param.26) | copy-start | bytes 3076
  141.4 45.7 %all-to-all-start.6 = ((bf16[32,16,1536]{2,1,0:T(8,128)(2,1)}), bf16[32,16,1536]{2,1,0:T(8,128)(2,1)S(1)}, u32[]{:S(2)}, u32[]{:S(2)}) async-start(bf16[32,16,1536]{2,1,0:T(8,128)(2,1)} %bitcast.21), calls=%async_computation.6 | async-start | bytes 3145728 | tf_op jit(solution)/shard_map/all_to_all | solution.py:20
  187.9 16.0 %all-to-all-start.7 = ((bf16[32,12,128]{2,1,0:T(8,128)(2,1)}), bf16[32,12,128]{2,1,0:T(8,128)(2,1)S(1)}, u32[]{:S(2)}, u32[]{:S(2)}) async-start(bf16[32,12,128]{2,1,0:T(8,128)(2,1)} %broadcast_in_dim.151), calls=%async_computation.7 | async-start | bytes 262144 | tf_op jit(solution)/shard_map/all_to_all | solution.py:20
  194.8 10.0 %copy-start.5 = (f32[1536]{0:T(1024)S(1)}, f32[1536]{0:T(1024)}, u32[]{:S(2)}) copy-start(f32[1536]{0:T(1024)} %param.28) | copy-start | bytes 18436
  207.3 9.5 %copy-start.1 = (bf16[63,1536]{1,0:T(8,128)(2,1)S(1)}, bf16[63,1536]{1,0:T(8,128)(2,1)}, u32[]{:S(2)}) copy-start(bf16[63,1536]{1,0:T(8,128)(2,1)} %param.25) | copy-start | bytes 580612
  212.0 14.5 %all-to-all-start.8 = ((bf16[32,12,128]{2,1,0:T(8,128)(2,1)}), bf16[32,12,128]{2,1,0:T(8,128)(2,1)S(1)}, u32[]{:S(2)}, u32[]{:S(2)}) async-start(bf16[32,12,128]{2,1,0:T(8,128)(2,1)} %reshape.251), calls=%async_computation.8 | async-start | bytes 262144 | tf_op jit(solution)/shard_map/all_to_all | solution.py:20
Sparse Core Ops, SparseCore 0:
  13.4 58.0 all-gather.3
